TPU v7x, 32 devices: a whole 2x2x4 slice. The times are simulated.
32 devices in a mesh: groups: 2 (over x), col: 16 (over z, y, core).
Axes of the slice: x: 2, y: 2, z: 4, core: 2. Of those that a mesh axis runs over, the one named last changes fastest.
Arguments:
- separator: float32 [32768, 16384], P(('groups', 'col')), parts along dimension 0, may hold values from -1 to 3.5, as said below
- pivots: bfloat16 [6, 512, 512], P('groups'), parts along dimension 0, may hold values from -1 to 2.5, as said below
- factor_sep: bfloat16 [6, 4096, 512], P('groups', 'col'), parts along dimension 0, may hold values from -0.8984375 to 0.8984375
- factor_window: bfloat16 [6, 512, 512], P('groups'), parts along dimension 0, may hold values from -0.25 to 0.25
- block_list: int32 [3, 32], replicated, may hold values from 0 to 127, as said below
Outputs:
- sep_columns: float32 [6, 16384, 512], P('groups', 'col'), parts along dimension 0
- window_inverse: float32 [6, 512, 1536], P('groups', 'col'), parts along dimension 0
There are 2 independent parts, one for each index of `groups`. A program takes and returns all parts, laid end to end along the dimension named above; an argument that names none is the same for every part. Nothing has to cross between parts.
Inputs may be any that keep to these rules, and one draw needn't show every extreme that they name: The separator is symmetric. Each pivots[k] is symmetric. `block_list`: each row names 32 different blocks in increasing order.
All inputs are finite; a program needn't handle non-finite values.
Results may differ from a plain program's by a relative error of at most 0.0003.
Values may be sent and summed in bfloat16 or wider, within the bound.
A program may use at most 320 MiB of HBM per device.

v0:
```python
import jax
import jax.numpy as jnp
from jax import lax
from jax.sharding import PartitionSpec as P

R = 16384
W = 512
BLOCK = 128
NB = 32
NSUP = 3


highest = lax.Precision.HIGHEST


def matmul(left_side, right_side):
    return jnp.dot(left_side, right_side, precision=highest, preferred_element_type=jnp.float32)


def inner_rows(left_side, right_side):
    return lax.dot_general(
        left_side,
        right_side,
        (((0,), (0,)), ((), ())),
        precision=highest,
        preferred_element_type=jnp.float32,
    )


def window_factor(factor_window, target, source):
    return factor_window[target * (target - 1) // 2 + source].astype(jnp.float32)


def local(separator, pivots, factor_sep, factor_window, block_list):
    local_rows = separator.shape[0]
    device = lax.axis_index("col")
    first_row = device * local_rows
    listed = NB * BLOCK
    blocked = separator.reshape(local_rows, R // BLOCK, BLOCK)
    chosen = jnp.take(blocked, block_list, axis=1)
    chosen = jnp.transpose(chosen, (1, 0, 2, 3)).reshape(NSUP, local_rows, listed)
    global_rows = first_row + jnp.arange(local_rows, dtype=jnp.int32)
    compressed = jnp.arange(listed, dtype=jnp.int32)
    target_rows = jnp.repeat(block_list, BLOCK, axis=1) * BLOCK + (compressed % BLOCK)[None, :]
    selector = (global_rows[None, :, None] == target_rows[:, None, :]).astype(jnp.bfloat16)
    share_rows = W // lax.axis_size("col")
    share_start = device * share_rows
    factor_piece = lax.all_gather(factor_sep, "col", axis=1, tiled=True)
    fold_direct = jnp.einsum(
        "krc,kcw->krw",
        chosen,
        factor_piece.astype(jnp.float32),
        precision=highest,
        preferred_element_type=jnp.float32,
    )
    located = jnp.einsum("krc,kcw->krw", selector, factor_piece, preferred_element_type=jnp.float32)
    columns = []
    window = [[None] * NSUP for position in range(NSUP)]
    for column in range(NSUP):
        direct = fold_direct[column]
        picked_rows = located[column]
        sep_image = direct
        for earlier in range(column):
            sep_image = sep_image + matmul(
                columns[earlier], window_factor(factor_window, column, earlier)
            )
        sep_column = -sep_image
        partials = [inner_rows(columns[earlier], picked_rows) for earlier in range(column)]
        partials.append(inner_rows(picked_rows, sep_column))
        pivot_now = pivots[column].astype(jnp.float32)
        totals = lax.psum(jnp.stack(partials), "col")
        for earlier in range(column):
            result = totals[earlier]
            for between in range(column):
                result = result + matmul(
                    window[earlier][between], window_factor(factor_window, column, between)
                )
            window[earlier][column] = -result
            window[column][earlier] = -result.T
        closing = totals[column]
        for earlier in range(column):
            closing = closing + inner_rows(
                window_factor(factor_window, column, earlier), window[earlier][column]
            )
        window[column][column] = pivot_now - closing
        columns.append(sep_column)
    sep_columns = jnp.stack(columns)
    window_rows = jnp.stack(
        [
            jnp.concatenate(
                [
                    lax.dynamic_slice_in_dim(window[position][between], share_start, share_rows, 0)
                    for between in range(NSUP)
                ],
                axis=1,
            )
            for position in range(NSUP)
        ]
    )
    return (sep_columns, window_rows)


def solution(mesh):
    return jax.shard_map(
        local,
        mesh=mesh,
        in_specs=(
            P(("groups", "col"), None),
            P("groups", None, None),
            P("groups", "col", None),
            P("groups", None, None),
            P(),
        ),
        out_specs=(P("groups", "col", None), P("groups", "col", None)),
        check_vma=False,
    )
```

profile of v0, /device:TPU:0, one launch (start us, length us, event | category | flops | bytes accessed | tf_op | source)
XLA Modules:
  0.0 445.2 jit_solution(2627646376404528957)
XLA Ops:
  8.7 66.0 %copy.15 = f32[1024,16384]{0,1:T(8,128)} copy(f32[1024,16384]{1,0:T(8,128)} %param.5) | data formatting | bytes 134217728 | tf_op args[0]
  74.8 65.9 %copy.16 = f32[1024,128,128]{2,0,1:T(8,128)} copy(f32[1024,128,128]{0,2,1:T(8,128)} %bitcast) | data formatting | bytes 134217728 | tf_op jit(solution)/shard_map/reshape | solution.py:39
  140.7 33.7 %gather_fusion = f32[96,1024,128]{2,1,0:T(8,128)} fusion(f32[1024,128,128]{2,0,1:T(8,128)} %copy.16, s32[1024]{0:T(1024)S(1)} %pad_clamp_fusion), kind=kCustom, calls=%fused_computation | custom fusion | bytes 100663680 | tf_op jit(solution)/shard_map/jit(_take)/gather | solution.py:40
  174.6 45.1 %fusion = f32[3,1024,512]{2,1,0:T(8,128)S(1)} fusion(bf16[3,4096,512]{2,1,0:T(8,128)(2,1)} %all-gather.2.cloned.1.call-done, f32[3,32,1024,128]{3,2,1,0:T(8,128)} %bitcast.178, pred[3,32]{1,0:T(4,128)(4,1)S(1)} %compare_and_fusion), kind=kOutput, calls=%fused_computation.1 | convolution fusion | flops 77321994240 | bytes 69206112 | tf_op jit(solution)/shard_map/krc,kcw->krw/dot_general | solution.py:49
  219.7 1.9 fusion.12
  221.6 1.8 fusion.51
  223.5 16.3 %fusion.3 = f32[3,1024,512]{2,1,0:T(8,128)S(1)} fusion(bf16[3,4096,512]{2,1,0:T(8,128)(2,1)} %all-gather.2.cloned.1.call-done, s32[3,4096]{1,0:T(4,128)S(1)} %bitcast_add_fusion, s32[1024]{0:T(1024)S(1)} %iota_add_fusion), kind=kOutput, calls=%fused_computation.5 | convolution fusion | flops 12897484800 | bytes 18927616 | tf_op jit(solution)/shard_map/krc,kcw->krw/dot_general | solution.py:56
  239.8 3.5 fusion.29
  243.3 3.5 fusion.35
  246.8 3.5 fusion.31
  250.3 12.3 %fusion.32 = f32[1,512,512]{2,1,0:T(8,128)S(1)} fusion(f32[3,1024,512]{2,1,0:T(8,128)S(1)} %fusion.3, f32[3,1024,512]{2,1,0:T(8,128)S(1)} %fusion), kind=kOutput, calls=%fused_computation.39 | convolution fusion | flops 3221749760 | bytes 5242880 | tf_op jit(solution)/shard_map/dot_general | solution.py:21
  262.7 4.5 %fusion.38 = f32[1,512,512]{2,1,0:T(8,128)} fusion(f32[3,1024,512]{2,1,0:T(8,128)S(1)} %fusion.3, f32[3,1024,512]{2,1,0:T(8,128)S(1)} %fusion), kind=kOutput, calls=%fused_computation.41 | convolution fusion | flops 3221749760 | bytes 5242880 | tf_op jit(solution)/shard_map/dot_general | solution.py:21
  267.2 2.0 fusion.10
  269.2 3.5 fusion.30
  272.8 1.6 pad_maximum_fusion.2
  274.3 2.0 pad_maximum_fusion.1
  277.5 2.0 slice_negate_fusion
  279.7 3.6 pad_maximum_fusion
  283.3 135.3 %all-reduce.3.cloned.1.call-done = (f32[2,512,512]{2,1,0:T(8,128)}, f32[1,512,512]{2,1,0:T(8,128)}, f32[3,512,512]{2,1,0:T(8,128)}) async-done(((f32[2,512,512]{2,1,0:T(8,128)}, f32[1,512,512]{2,1,0:T(8,128)}, f32[3,512,512]{2,1,0:T(8,128)}), (f32[2,512,512]{2,1,0:T(8,128)}, f32[1,512,512]{2,1,0:T(8,128)}, f32[3,512,512]{2,1,0:T(8,128)})) %all-reduce.3.cloned.1.call-update) | async-done | bytes 6291472 | tf_op jit(solution)/shard_map/psum | solution.py:71
  418.6 1.5 convert_subtract_fusion
  420.1 2.4 fusion.43
  422.5 2.3 fusion.45
  429.1 2.1 convolution_bitcast_fusion.1
  432.8 2.1 convolution_bitcast_fusion
  (50 shorter events, 12.2 us)
Async XLA Ops:
  7.2 167.4 %all-gather.2.cloned.1.call-start = ((), (), s32[]{:S(2)}) async-start(), calls=%async_computation | async-start | bytes 13369344 | tf_op jit(solution)/shard_map/all_gather | solution.py:48
  7.9 410.7 %all-reduce.3.cloned.1.call-start = ((), (), s32[]{:S(2)}) async-start(), calls=%async_computation.1 | async-start | bytes 12582912 | tf_op jit(solution)/shard_map/psum | solution.py:71
  140.7 33.7 %copy-start.8 = (s32[3,32]{1,0:T(4,128)S(1)}, s32[3,32]{1,0:T(4,128)}, u32[]{:S(2)}) copy-start(s32[3,32]{1,0:T(4,128)} %param.9) | copy-start | bytes 1156
  174.6 45.1 %copy-start.1 = (bf16[3,512,512]{2,1,0:T(8,128)(2,1)S(1)}, bf16[3,512,512]{2,1,0:T(8,128)(2,1)}, u32[]{:S(2)}) copy-start(bf16[3,512,512]{2,1,0:T(8,128)(2,1)} %param.8) | copy-start | bytes 4718596
  219.7 47.5 %copy-start = (f32[3,1024,512]{2,1,0:T(8,128)}, f32[3,1024,512]{2,1,0:T(8,128)S(1)}, u32[]{:S(2)}) copy-start(f32[3,1024,512]{2,1,0:T(8,128)S(1)} %fusion) | copy-start | bytes 18874372
  269.2 3.5 copy-start.3
  277.4 2.2 copy-start.4
  283.3 136.8 %copy-start.2 = (bf16[3,512,512]{2,1,0:T(8,128)(2,1)S(1)}, bf16[3,512,512]{2,1,0:T(8,128)(2,1)}, u32[]{:S(2)}) copy-start(bf16[3,512,512]{2,1,0:T(8,128)(2,1)} %param.8) | copy-start | bytes 4718596
  420.1 2.4 copy-start.6
  422.5 2.3 copy-start.5
  434.9 2.3 copy-start.7
Sparse Core Ops, SparseCore 0:
  10.2 103.1 all-gather.1
  276.5 142.0 all-reduce.2
where the time goes:
time: 450 us; the launch traced here: 445 us
  local copies, waits for them, and re-layouts  170 us (38%)
  waiting for transfers between devices  136 us (30%)
  matrix products  111 us (25%)
  between operations  14.6 us (3%)
  other arithmetic  14.1 us (3%)
    psum x1, waiting for transfers between devices, local(): totals = lax.psum(jnp.stack(partials), 'col')  135 us
    unnamed x21, local copies, waits for them, and re-layouts  67.5 us
    reshape x1, local copies, waits for them, and re-layouts, local(): blocked = separator.reshape(local_rows, R // BLOCK, BLOCK)  65.9 us
    dot_general x1, matrix products, local(): jnp.einsum('krc,kcw->krw', chosen, factor_piece.astype(jnp.float32), prec...  45.1 us
    dot_general x9, matrix products, inner_rows(): lax.dot_general(left_side, right_side, (((0,), (0,)), ((), ())), precisio...  37.3 us
    gather x1, local copies, waits for them, and re-layouts, local(): chosen = jnp.take(blocked, block_list, axis=1)  33.7 us
    dot_general x1, matrix products, local(): jnp.einsum('krc,kcw->krw', selector, factor_piece, preferred_element_type...  16.3 us
    dot_general x8, matrix products, matmul(): jnp.dot(left_side, right_side, precision=highest, preferred_element_type=...  12.1 us
  transfers between devices with their start and end apart: 2, of which 1 were waited for; matrix products, arithmetic and copies ran while one was open for 39% of the time, Pallas kernels for 0%

commit v1 on v0

v1 whole, which is shorter than its diff:
```python
import functools

import jax
import jax.numpy as jnp
from jax import lax
from jax.experimental import pallas as pl
from jax.experimental.pallas import tpu as pltpu
from jax.sharding import PartitionSpec as P

STEP_BLOCKS = 4
F32 = jnp.float32


def split(value):
    high = value.astype(jnp.bfloat16)
    low = (value - high.astype(F32)).astype(jnp.bfloat16)
    return high, low


def split_whole(value):
    high = lax.reduce_precision(value, 8, 7)
    return high.astype(jnp.bfloat16), (value - high).astype(jnp.bfloat16)


def dot_split(left, right, dims=(((1,), (0,)), ((), ())), cut=split):
    high, low = cut(left)
    return lax.dot_general(high, right, dims, preferred_element_type=F32) + lax.dot_general(
        low, right, dims, preferred_element_type=F32
    )


def fold_kernel(per_step, n_earlier, list_ref, *refs):
    blocks = refs[:per_step]
    factor_ref = refs[per_step]
    earlier = refs[per_step + 1 : per_step + 1 + n_earlier]
    window = refs[per_step + 1 + n_earlier : per_step + 1 + 2 * n_earlier]
    out_ref = refs[-1]
    step = pl.program_id(0)
    left = jnp.concatenate([block[...] for block in blocks], axis=1)
    total = dot_split(left, factor_ref[...])

    @pl.when(step == 0)
    def _():
        start = total
        for column_ref, window_ref in zip(earlier, window):
            start = start + dot_split(column_ref[...], window_ref[...])
        out_ref[...] = -start

    @pl.when(step > 0)
    def _():
        out_ref[...] -= total


def fold(separator, listed, factor, earlier, window, block):
    rows = separator.shape[0]
    width = factor.shape[1]
    count = listed.shape[0]
    per_step = min(STEP_BLOCKS, count)
    n_earlier = len(earlier)

    def picked(i):
        return pl.BlockSpec((rows, block), lambda s, lst, i=i: (0, lst[s * per_step + i]))

    whole = lambda shape: pl.BlockSpec(shape, lambda s, lst: (0, 0))
    return pl.pallas_call(
        functools.partial(fold_kernel, per_step, n_earlier),
        grid_spec=pltpu.PrefetchScalarGridSpec(
            num_scalar_prefetch=1,
            grid=(count // per_step,),
            in_specs=[picked(i) for i in range(per_step)]
            + [pl.BlockSpec((per_step * block, width), lambda s, lst: (s, 0))]
            + [whole((rows, width))] * n_earlier
            + [whole((width, width))] * n_earlier,
            out_specs=whole((rows, width)),
        ),
        out_shape=jax.ShapeDtypeStruct((rows, width), F32),
        compiler_params=pltpu.CompilerParams(vmem_limit_bytes=48 * 1024 * 1024),
        name="fold",
    )(listed, *([separator] * per_step), factor, *earlier, *window)


def couple_kernel(n_columns, place_ref, present_ref, factor_ref, *refs):
    columns = refs[:n_columns]
    out_ref = refs[n_columns]
    step = pl.program_id(0)

    @pl.when(step == 0)
    def _():
        out_ref[...] = jnp.zeros_like(out_ref)

    @pl.when(present_ref[step] > 0)
    def _():
        factor = factor_ref[...]
        for j in range(n_columns):
            out_ref[j] += dot_split(columns[j][...], factor, (((0,), (0,)), ((), ())))


def couple(place, present, factor, columns, block):
    rows, width = columns[0].shape
    n_columns = len(columns)
    return pl.pallas_call(
        functools.partial(couple_kernel, n_columns),
        grid_spec=pltpu.PrefetchScalarGridSpec(
            num_scalar_prefetch=2,
            grid=(rows // block,),
            in_specs=[pl.BlockSpec((block, width), lambda s, place, present: (place[s], 0))]
            + [pl.BlockSpec((block, width), lambda s, place, present: (s, 0))] * n_columns,
            out_specs=pl.BlockSpec((n_columns, width, width), lambda s, place, present: (0, 0, 0)),
        ),
        out_shape=jax.ShapeDtypeStruct((n_columns, width, width), F32),
        compiler_params=pltpu.CompilerParams(vmem_limit_bytes=48 * 1024 * 1024),
        name="couple",
    )(place, present, factor, *columns)


def local(separator, pivots, factor_sep, factor_window, block_list):
    n_sup, count = block_list.shape
    n_dev = lax.axis_size("col")
    block = factor_sep.shape[1] * n_dev // count
    local_rows = separator.shape[0]
    width = pivots.shape[1]
    local_blocks = local_rows // block
    device = lax.axis_index("col")
    share = width // n_dev
    share_start = device * share

    def between(target, source):
        return factor_window[target * (target - 1) // 2 + source]

    factors = [lax.all_gather(factor_sep[k], "col", axis=0, tiled=True) for k in range(n_sup)]

    own = device * local_blocks + jnp.arange(local_blocks, dtype=jnp.int32)
    match = block_list[:, None, :] == own[None, :, None]
    present = jnp.any(match, axis=2).astype(jnp.int32)
    place = jnp.sum(jnp.where(match, jnp.arange(count, dtype=jnp.int32)[None, None, :], 0), axis=2).astype(jnp.int32)

    base = [[None] * n_sup for _ in range(n_sup)]
    for k in range(n_sup):
        for j in range(k + 1):
            total = pivots[k].astype(F32) if j == k else jnp.zeros((width, width), F32)
            for i in range(k):
                total = total - dot_split(base[j][i], between(k, i), cut=split_whole)
            base[j][k] = total
            base[k][j] = total.T

    columns = []
    sums = [[None] * n_sup for _ in range(n_sup)]
    scattered = {}
    pending = []
    for k in range(n_sup):
        columns.append(
            fold(separator, block_list[k], factors[k], columns[:], [between(k, j) for j in range(k)], block)
        )
        raw = couple(place[k], present[k], factors[k], columns, block)
        for j in range(k):
            sums[k][j] = couple(place[j], present[j], factors[j], [columns[k]], block)[0]
        for i in range(k):
            for j in range(i):
                sums[k][i] = sums[k][i] - dot_split(sums[k][j], between(i, j), cut=split_whole)
        for j in range(k + 1):
            total = raw[j]
            for i in range(k):
                total = total - dot_split(sums[j][i], between(k, i), cut=split_whole)
            sums[j][k] = total
            pending.append((j, k))
        if k >= n_sup - 2:
            mine = lax.psum_scatter(
                jnp.stack([sums[j][i] for j, i in pending]), "col", scatter_dimension=1, tiled=True
            )
            for at, pair in enumerate(pending):
                scattered[pair] = mine[at]
            pending = []

    result = [[None] * n_sup for _ in range(n_sup)]
    upper = []
    for k in range(n_sup):
        for j in range(k + 1):
            result[j][k] = lax.dynamic_slice_in_dim(base[j][k], share_start, share, 0) - scattered[(j, k)]
            if j < k:
                upper.append((j, k))
    swapped = lax.all_to_all(
        jnp.stack([result[j][k] for j, k in upper]), "col", split_axis=2, concat_axis=1, tiled=True
    )
    for at, (j, k) in enumerate(upper):
        result[k][j] = swapped[at].T
    window_rows = jnp.stack([jnp.concatenate(row, axis=1) for row in result])
    return jnp.stack(columns), window_rows


def solution(mesh):
    return jax.shard_map(
        local,
        mesh=mesh,
        in_specs=(
            P(("groups", "col"), None),
            P("groups", None, None),
            P("groups", "col", None),
            P("groups", None, None),
            P(),
        ),
        out_specs=(P("groups", "col", None), P("groups", "col", None)),
        check_vma=False,
    )
```

time: 450 us -> 333 us (0.74)
  local copies, waits for them, and re-layouts: 170 us -> 21.3 us
  matrix products: 111 us -> 25.3 us
  Pallas kernels: 0 us -> 77.2 us
  waiting for transfers between devices: 136 us -> 171 us
    psum x1 -> x0, waiting for transfers between devices: 135 us -> none  [local(): totals = lax.psum(jnp.stack(partials), 'col')]
    all_gather x1 -> x3, waiting for transfers between devices: 0.02 us -> 92.4 us  [local(): lax.all_gather(factor_sep[k], 'col', axis=0, tiled=True)]
    dot_general x19 -> x34, matrix products: 111 us -> 25.3 us  [the longest x17 13.2 us: dot_split(): lax.dot_general(high, right, dims, preferred_element_type=F32)]
    pallas_call x0 -> x9, Pallas kernels: none -> 77.2 us  [the longest x3 49.7 us: fold(): pl.pallas_call(functools.partial(fold_kernel, per_step, n_earlier), grid_...]
    reduce_scatter x0 -> x2, waiting for transfers between devices: none -> 74.6 us  [local(): lax.psum_scatter(jnp.stack([sums[j][i] for j, i in pending]), 'col', scat...]
    reshape x1 -> x0, local copies, waits for them, and re-layouts: 65.9 us -> none  [local(): blocked = separator.reshape(local_rows, R // BLOCK, BLOCK)]
    unnamed x21 -> x56, local copies, waits for them, and re-layouts: 67.5 us -> 15 us
    gather x1 -> x0, local copies, waits for them, and re-layouts: 33.7 us -> none  [local(): chosen = jnp.take(blocked, block_list, axis=1)]
  transfers between devices with their start and end apart: 2 -> 6, of which waited for: 1 -> 6; matrix products, arithmetic and copies ran while one was open for 39% -> 14% of each run, Pallas kernels for 0% -> 23%
where the time goes in v1:
time: 333 us; the launch traced here: 331 us
  waiting for transfers between devices  171 us (51%)
  Pallas kernels  77.2 us (23%)
  matrix products  25.3 us (8%)
  local copies, waits for them, and re-layouts  21.3 us (6%)
  other arithmetic  16.8 us (5%)
  between operations  14.4 us (4%)
  starting transfers between devices  4.17 us (1%)
    all_gather x3, waiting for transfers between devices, local(): lax.all_gather(factor_sep[k], 'col', axis=0, tiled=True)  92.4 us
    reduce_scatter x2, waiting for transfers between devices, local(): lax.psum_scatter(jnp.stack([sums[j][i] for j, i in pending]), 'col', scat...  74.6 us
    pallas_call x3, Pallas kernels, fold(): pl.pallas_call(functools.partial(fold_kernel, per_step, n_earlier), grid_...  49.7 us
    pallas_call x6, Pallas kernels, couple(): pl.pallas_call(functools.partial(couple_kernel, n_columns), grid_spec=plt...  27.5 us
    unnamed x56, local copies, waits for them, and re-layouts  15 us
    dot_general x17, matrix products, dot_split(): lax.dot_general(high, right, dims, preferred_element_type=F32)  13.2 us
    dot_general x17, matrix products, dot_split(): lax.dot_general(low, right, dims, preferred_element_type=F32)  12.2 us
  transfers between devices with their start and end apart: 6, of which 6 were waited for; matrix products, arithmetic and copies ran while one was open for 14% of the time, Pallas kernels for 23%

profile of v1, /device:TPU:0, one launch (start us, length us, event | category | flops | bytes accessed | tf_op | source)
XLA Modules:
  0.0 330.6 jit_solution(3803493205673508785)
XLA Ops:
  7.2 2.1 fusion.93
  14.8 48.5 %all-gather.7.cloned.1.call-done = bf16[1,4096,512]{2,1,0:T(8,128)(2,1)} async-done(((bf16[1,256,512]{2,1,0:T(8,128)(2,1)}), bf16[1,4096,512]{2,1,0:T(8,128)(2,1)}) %all-gather.7.cloned.1.call-update) | async-done | bytes 4194320 | tf_op jit(solution)/shard_map/all_gather | solution.py:130
  63.3 15.0 %fold.3.refs_5_.refs_0_ = f32[1024,512]{1,0:T(8,128)S(1)} custom-call(s32[32]{0:T(128)S(1)} %get-tuple-element.27.list_ref, f32[1024,16384]{1,0:T(8,128)} %refs_3_.5, f32[1024,16384]{1,0:T(8,128)} %refs_3_.5, f32[1024,16384]{1,0:T(8,128)} %refs_3_.5, f32[1024,16384]{1,0:T(8,128)} %refs_3_.5, bf16[4096,512]{1,0:T(8,128)(2,1)} %bitcast.221), custom_call_target="tpu_custom_call" | custom-call | tf_op jit(solution)/shard_map/fold/pallas_call | solution.py:65
  78.3 3.5 %couple.6 = f32[1,512,512]{2,1,0:T(8,128)S(1)} custom-call(s32[8]{0:T(128)S(1)} %get-tuple-element.29.place_ref, s32[8]{0:T(128)S(1)} %get-tuple-element.22.present_ref, bf16[4096,512]{1,0:T(8,128)(2,1)} %bitcast.222, f32[1024,512]{1,0:T(8,128)S(1)} %fold.3.refs_5_.refs_0_), custom_call_target="tpu_custom_call" | custom-call | tf_op jit(solution)/shard_map/couple/pallas_call | solution.py:101
  81.8 32.6 %all-gather.9.cloned.1.call-done = bf16[1,4096,512]{2,1,0:T(8,128)(2,1)} async-done(((bf16[1,256,512]{2,1,0:T(8,128)(2,1)}), bf16[1,4096,512]{2,1,0:T(8,128)(2,1)}) %all-gather.9.cloned.1.call-update) | async-done | bytes 4194320 | tf_op jit(solution)/shard_map/all_gather | solution.py:130
  115.4 16.1 %fold.4.refs_6_.refs_1_.refs_0_ = f32[1024,512]{1,0:T(8,128)S(1)} custom-call(s32[32]{0:T(128)S(1)} %get-tuple-element.26.list_ref, f32[1024,16384]{1,0:T(8,128)} %refs_3_.5, f32[1024,16384]{1,0:T(8,128)} %refs_3_.5, f32[1024,16384]{1,0:T(8,128)} %refs_3_.5, f32[1024,16384]{1,0:T(8,128)} %refs_3_.5, bf16[4096,512]{1,0:T(8,128)(2,1)} %bitcast.225, ...), custom_call_target="tpu_custom_call" | custom-call | tf_op jit(solution)/shard_map/fold/pallas_call | solution.py:65
  131.6 3.7 %couple.8 = f32[1,512,512]{2,1,0:T(8,128)S(1)} custom-call(s32[8]{0:T(128)S(1)} %get-tuple-element.29.place_ref, s32[8]{0:T(128)S(1)} %get-tuple-element.22.present_ref, bf16[4096,512]{1,0:T(8,128)(2,1)} %bitcast.223, f32[1024,512]{1,0:T(8,128)S(1)} %fold.4.refs_6_.refs_1_.refs_0_), custom_call_target="tpu_custom_call" | custom-call | tf_op jit(solution)/shard_map/couple/pallas_call | solution.py:101
  135.3 5.7 %couple.7 = f32[2,512,512]{2,1,0:T(8,128)S(1)} custom-call(s32[8]{0:T(128)S(1)} %get-tuple-element.31.place_ref, s32[8]{0:T(128)S(1)} %get-tuple-element.20.present_ref, bf16[4096,512]{1,0:T(8,128)(2,1)} %bitcast.226, f32[1024,512]{1,0:T(8,128)S(1)} %fold.3.refs_5_.refs_0_, f32[1024,512]{1,0:T(8,128)} %copy-done), custom_call_target="tpu_custom_call" | custom-call | tf_op jit(solution)/shard_map/couple/pallas_call | solution.py:101
  143.9 1.9 pad_maximum_fusion.1
  147.2 2.1 copy.23
  149.4 2.1 copy.24
  151.5 2.6 fusion.53
  154.1 11.4 %all-gather.11.cloned.1.call-done = bf16[1,4096,512]{2,1,0:T(8,128)(2,1)} async-done(((bf16[1,256,512]{2,1,0:T(8,128)(2,1)}), bf16[1,4096,512]{2,1,0:T(8,128)(2,1)}) %all-gather.11.cloned.1.call-update) | async-done | bytes 4194320 | tf_op jit(solution)/shard_map/all_gather | solution.py:130
  167.6 18.6 %fold.5.refs_2_.refs_0_ = f32[1024,512]{1,0:T(8,128)S(1)} custom-call(s32[32]{0:T(128)S(1)} %get-tuple-element.28.list_ref, f32[1024,16384]{1,0:T(8,128)} %refs_3_.5, f32[1024,16384]{1,0:T(8,128)} %refs_3_.5, f32[1024,16384]{1,0:T(8,128)} %refs_3_.5, f32[1024,16384]{1,0:T(8,128)} %refs_3_.5, bf16[4096,512]{1,0:T(8,128)(2,1)} %bitcast.228, ...), custom_call_target="tpu_custom_call" | custom-call | tf_op jit(solution)/shard_map/fold/pallas_call | solution.py:65
  186.2 3.7 %couple.10 = f32[1,512,512]{2,1,0:T(8,128)S(1)} custom-call(s32[8]{0:T(128)S(1)} %get-tuple-element.29.place_ref, s32[8]{0:T(128)S(1)} %get-tuple-element.22.present_ref, bf16[4096,512]{1,0:T(8,128)(2,1)} %bitcast.224, f32[1024,512]{1,0:T(8,128)S(1)} %fold.5.refs_2_.refs_0_), custom_call_target="tpu_custom_call" | custom-call | tf_op jit(solution)/shard_map/couple/pallas_call | solution.py:101
  189.9 2.3 couple.11
  192.2 8.5 %couple.9 = f32[3,512,512]{2,1,0:T(8,128)} custom-call(s32[8]{0:T(128)S(1)} %get-tuple-element.30.place_ref, s32[8]{0:T(128)S(1)} %get-tuple-element.21.present_ref, bf16[4096,512]{1,0:T(8,128)(2,1)} %bitcast.229, f32[1024,512]{1,0:T(8,128)S(1)} %fold.3.refs_5_.refs_0_, f32[1024,512]{1,0:T(8,128)S(1)} %copy-done.1, f32[1024,512]{1,0:T(8,128)} %copy-done.2), custom_call_target="tpu_custom_call" | custom-call | tf_op jit(solution)/shard_map/couple/pallas_call | solution.py:101
  209.9 2.0 pad_maximum_fusion.2
  213.8 1.9 fusion.15
  227.4 6.7 %reduce-scatter.3.cloned.1.call-done = f32[3,32,512]{2,1,0:T(8,128)} async-done(((f32[3,512,512]{2,1,0:T(8,128)}), f32[3,32,512]{2,1,0:T(8,128)}) %reduce-scatter.3.cloned.1.call-update) | async-done | bytes 196624 | tf_op jit(solution)/shard_map/reduce_scatter | solution.py:167
  235.7 67.9 %reduce-scatter.5.cloned.1.call-done = f32[3,32,512]{2,1,0:T(8,128)} async-done(((f32[3,512,512]{2,1,0:T(8,128)}), f32[3,32,512]{2,1,0:T(8,128)}) %reduce-scatter.5.cloned.1.call-update) | async-done | bytes 196624 | tf_op jit(solution)/shard_map/reduce_scatter | solution.py:167
  307.1 3.8 %all-to-all-start = ((f32[16,1,3072]{2,1,0:T(1,128)}), f32[16,1,3072]{2,1,0:T(1,128)S(1)}, u32[]{:S(2)}, u32[]{:S(2)}) async-start(f32[16,1,3072]{2,1,0:T(1,128)} %reshape.41), calls=%async_computation.2 | async-start | bytes 393216 | tf_op jit(solution)/shard_map/all_to_all | solution.py:181
  310.9 5.7 %pad_maximum_fusion = f32[3,1024,512]{2,1,0:T(8,128)} fusion(f32[1,1024,512]{2,1,0:T(8,128)} %bitcast.220, f32[1,1024,512]{2,1,0:T(8,128)} %bitcast.219, f32[1,1024,512]{2,1,0:T(8,128)S(1)} %bitcast.218), kind=kLoop, calls=%fused_computation | loop fusion | flops 3145728 | bytes 12582912 | tf_op jit(solution)/shard_map/stack | solution.py:187
  316.6 3.0 all-to-all-done
  (121 shorter events, 44.8 us)
Async XLA Ops:
  7.2 3.8 %copy-start.25 = (s32[3,32]{1,0:T(4,128)S(1)}, s32[3,32]{1,0:T(4,128)}, u32[]{:S(2)}) copy-start(s32[3,32]{1,0:T(4,128)} %param.9) | copy-start | bytes 1156
  7.2 4.3 %copy-start.8 = (bf16[3,512,512]{2,1,0:T(8,128)(2,1)S(1)}, bf16[3,512,512]{2,1,0:T(8,128)(2,1)}, u32[]{:S(2)}) copy-start(bf16[3,512,512]{2,1,0:T(8,128)(2,1)} %param.8) | copy-start | bytes 4718596
  7.2 56.1 %all-gather.7.cloned.1.call-start = ((), (), s32[]{:S(2)}) async-start(), calls=%async_computation.5 | async-start | bytes 4456448 | tf_op jit(solution)/shard_map/all_gather | solution.py:130
  9.4 105.0 %all-gather.9.cloned.1.call-start = ((), (), s32[]{:S(2)}) async-start(), calls=%async_computation.6 | async-start | bytes 4456448 | tf_op jit(solution)/shard_map/all_gather | solution.py:130
  10.2 155.3 %all-gather.11.cloned.1.call-start = ((), (), s32[]{:S(2)}) async-start(), calls=%async_computation.7 | async-start | bytes 4456448 | tf_op jit(solution)/shard_map/all_gather | solution.py:130
  10.9 223.2 %reduce-scatter.3.cloned.1.call-start = ((), (), s32[]{:S(2)}) async-start(), calls=%async_computation.3 | async-start | bytes 3342336 | tf_op jit(solution)/shard_map/reduce_scatter | solution.py:167
  11.4 2.0 copy-start.20
  131.6 3.7 %copy-start = (f32[1024,512]{1,0:T(8,128)}, f32[1024,512]{1,0:T(8,128)S(1)}, u32[]{:S(2)}) copy-start(f32[1024,512]{1,0:T(8,128)S(1)} %fold.4.refs_6_.refs_1_.refs_0_) | copy-start | bytes 6291460
  135.3 6.7 %copy-start.3 = (f32[1,512,512]{2,1,0:T(8,128)}, f32[1,512,512]{2,1,0:T(8,128)S(1)}, u32[]{:S(2)}) copy-start(f32[1,512,512]{2,1,0:T(8,128)S(1)} %couple.8) | copy-start | bytes 3145732
  135.3 5.8 %copy-start.9 = (bf16[3,512,512]{2,1,0:T(8,128)(2,1)S(1)}, bf16[3,512,512]{2,1,0:T(8,128)(2,1)}, u32[]{:S(2)}) copy-start(bf16[3,512,512]{2,1,0:T(8,128)(2,1)} %param.8) | copy-start | bytes 4718596
  145.9 157.7 %reduce-scatter.5.cloned.1.call-start = ((), (), s32[]{:S(2)}) async-start(), calls=%async_computation.4 | async-start | bytes 3342336 | tf_op jit(solution)/shard_map/reduce_scatter | solution.py:167
  186.2 3.7 %copy-start.2 = (f32[1024,512]{1,0:T(8,128)}, f32[1024,512]{1,0:T(8,128)S(1)}, u32[]{:S(2)}) copy-start(f32[1024,512]{1,0:T(8,128)S(1)} %fold.5.refs_2_.refs_0_) | copy-start | bytes 6291460
  189.9 2.3 copy-start.1
  192.2 8.5 %copy-start.10 = (bf16[3,512,512]{2,1,0:T(8,128)(2,1)S(1)}, bf16[3,512,512]{2,1,0:T(8,128)(2,1)}, u32[]{:S(2)}) copy-start(bf16[3,512,512]{2,1,0:T(8,128)(2,1)} %param.8) | copy-start | bytes 4718596
  200.8 1.2 copy-start.15
  200.8 2.2 copy-start.16
  203.5 1.2 copy-start.13
  204.7 1.2 copy-start.4
  211.9 1.8 copy-start.11
  216.1 1.0 copy-start.21
  219.1 2.9 copy-start.17
  224.4 1.5 copy-start.18
  307.1 12.5 %all-to-all-start = ((f32[16,1,3072]{2,1,0:T(1,128)}), f32[16,1,3072]{2,1,0:T(1,128)S(1)}, u32[]{:S(2)}, u32[]{:S(2)}) async-start(f32[16,1,3072]{2,1,0:T(1,128)} %reshape.41), calls=%async_computation.2 | async-start | bytes 393216 | tf_op jit(solution)/shard_map/all_to_all | solution.py:181
  310.9 5.7 %copy-start.24 = (f32[32,512]{1,0:T(8,128)S(1)}, f32[32,512]{1,0:T(8,128)}, u32[]{:S(2)}) copy-start(f32[32,512]{1,0:T(8,128)} %get-tuple-element.14) | copy-start | bytes 196612
  (8 other events, 7.8 us)
Sparse Core Ops, SparseCore 0:
  10.2 53.0 all-gather.6
  65.4 48.8 all-gather.8
  116.6 48.8 all-gather.10
  169.1 64.9 reduce-scatter.2
  238.4 65.2 reduce-scatter.4

commit v2 on v1

--- a/solution.py
+++ b/solution.py
@@ -51,9 +51,9 @@
         out_ref[...] -= total
 
 
-def fold(separator, listed, factor, earlier, window, block):
+def fold(separator, listed, factor, which, earlier, window, block):
     rows = separator.shape[0]
-    width = factor.shape[1]
+    width = factor.shape[2]
     count = listed.shape[0]
     per_step = min(STEP_BLOCKS, count)
     n_earlier = len(earlier)
@@ -68,7 +68,7 @@
             num_scalar_prefetch=1,
             grid=(count // per_step,),
             in_specs=[picked(i) for i in range(per_step)]
-            + [pl.BlockSpec((per_step * block, width), lambda s, lst: (s, 0))]
+            + [pl.BlockSpec((None, per_step * block, width), lambda s, lst: (which, s, 0))]
             + [whole((rows, width))] * n_earlier
             + [whole((width, width))] * n_earlier,
             out_specs=whole((rows, width)),
@@ -95,7 +95,7 @@
             out_ref[j] += dot_split(columns[j][...], factor, (((0,), (0,)), ((), ())))
 
 
-def couple(place, present, factor, columns, block):
+def couple(place, present, factor, which, columns, block):
     rows, width = columns[0].shape
     n_columns = len(columns)
     return pl.pallas_call(
@@ -103,7 +103,7 @@
         grid_spec=pltpu.PrefetchScalarGridSpec(
             num_scalar_prefetch=2,
             grid=(rows // block,),
-            in_specs=[pl.BlockSpec((block, width), lambda s, place, present: (place[s], 0))]
+            in_specs=[pl.BlockSpec((None, block, width), lambda s, place, present: (which, place[s], 0))]
             + [pl.BlockSpec((block, width), lambda s, place, present: (s, 0))] * n_columns,
             out_specs=pl.BlockSpec((n_columns, width, width), lambda s, place, present: (0, 0, 0)),
         ),
@@ -111,6 +111,26 @@
         compiler_params=pltpu.CompilerParams(vmem_limit_bytes=48 * 1024 * 1024),
         name="couple",
     )(place, present, factor, *columns)
+
+
+def halving_scatter(value, n_dev):
+    if n_dev & (n_dev - 1):
+        return lax.psum_scatter(value, "col", scatter_dimension=1, tiled=True)
+    count, rows, width = value.shape
+    share = rows // n_dev
+    device = lax.axis_index("col")
+    held = n_dev
+    stage = 1
+    while held > 1:
+        held //= 2
+        parts = value.reshape(count, held, 2, share, width)
+        bit = (device // stage) % 2
+        kept = lax.dynamic_index_in_dim(parts, bit, 2, keepdims=False)
+        sent = lax.dynamic_index_in_dim(parts, 1 - bit, 2, keepdims=False)
+        got = lax.ppermute(sent, "col", [(i, i ^ stage) for i in range(n_dev)])
+        value = kept + got
+        stage *= 2
+    return value.reshape(count, share, width)
 
 
 def local(separator, pivots, factor_sep, factor_window, block_list):
@@ -127,7 +147,7 @@
     def between(target, source):
         return factor_window[target * (target - 1) // 2 + source]
 
-    factors = [lax.all_gather(factor_sep[k], "col", axis=0, tiled=True) for k in range(n_sup)]
+    factors = lax.all_gather(factor_sep, "col", axis=1, tiled=True)
 
     own = device * local_blocks + jnp.arange(local_blocks, dtype=jnp.int32)
     match = block_list[:, None, :] == own[None, :, None]
@@ -149,11 +169,11 @@
     pending = []
     for k in range(n_sup):
         columns.append(
-            fold(separator, block_list[k], factors[k], columns[:], [between(k, j) for j in range(k)], block)
+            fold(separator, block_list[k], factors, k, columns[:], [between(k, j) for j in range(k)], block)
         )
-        raw = couple(place[k], present[k], factors[k], columns, block)
+        raw = couple(place[k], present[k], factors, k, columns, block)
         for j in range(k):
-            sums[k][j] = couple(place[j], present[j], factors[j], [columns[k]], block)[0]
+            sums[k][j] = couple(place[j], present[j], factors, j, [columns[k]], block)[0]
         for i in range(k):
             for j in range(i):
                 sums[k][i] = sums[k][i] - dot_split(sums[k][j], between(i, j), cut=split_whole)
@@ -164,9 +184,7 @@
             sums[j][k] = total
             pending.append((j, k))
         if k >= n_sup - 2:
-            mine = lax.psum_scatter(
-                jnp.stack([sums[j][i] for j, i in pending]), "col", scatter_dimension=1, tiled=True
-            )
+            mine = halving_scatter(jnp.stack([sums[j][i] for j, i in pending]), n_dev)
             for at, pair in enumerate(pending):
                 scattered[pair] = mine[at]
             pending = []

time: 333 us -> 325 us (0.976); the launches traced: 331 us -> 326 us
  waiting for transfers between devices: 171 us -> 129 us
  starting transfers between devices: 4.17 us -> 26.1 us
  matrix products: 25.3 us -> 31.9 us
  other arithmetic: 16.8 us -> 23.4 us
    reduce_scatter x2 -> x0, waiting for transfers between devices: 74.6 us -> none  [local(): lax.psum_scatter(jnp.stack([sums[j][i] for j, i in pending]), 'col', scat...]
    ppermute x0 -> x8, waiting for transfers between devices: none -> 34.3 us  [halving_scatter(): got = lax.ppermute(sent, 'col', [(i, i ^ stage) for i in range(n_dev)])]
    ppermute x0 -> x8, starting transfers between devices: none -> 22.1 us  [halving_scatter(): got = lax.ppermute(sent, 'col', [(i, i ^ stage) for i in range(n_dev)])]
    add x0 -> x8, other arithmetic: none -> 7.49 us  [halving_scatter(): value = kept + got]
    squeeze x1 -> x9, local copies, waits for them, and re-layouts: 0.01 us -> 5.2 us  [the longest x8 5.19 us: halving_scatter(): sent = lax.dynamic_index_in_dim(parts, 1 - bit, 2, keepdims=False)]
    dot_general x17, matrix products: 13.2 us -> 17 us  [dot_split(): lax.dot_general(high, right, dims, preferred_element_type=F32)]
    unnamed x56 -> x74, local copies, waits for them, and re-layouts: 15 us -> 12.6 us
    all_gather x3 -> x1, waiting for transfers between devices: 92.4 us -> 91.3 us  [local(): factors = lax.all_gather(factor_sep, 'col', axis=1, tiled=True)]
  transfers between devices with their start and end apart: 6 -> 10, of which waited for: 6 -> 5; matrix products, arithmetic and copies ran while one was open for 14% -> 15% of each run, Pallas kernels for 23% -> 4%
where the time goes in v2:
time: 325 us; the launch traced here: 326 us
  waiting for transfers between devices  129 us (40%)
  Pallas kernels  78.7 us (24%)
  matrix products  31.9 us (10%)
  starting transfers between devices  26.1 us (8%)
  other arithmetic  23.4 us (7%)
  local copies, waits for them, and re-layouts  21.7 us (7%)
  between operations  14.8 us (5%)
    all_gather x1, waiting for transfers between devices, local(): factors = lax.all_gather(factor_sep, 'col', axis=1, tiled=True)  91.3 us
    pallas_call x3, Pallas kernels, fold(): pl.pallas_call(functools.partial(fold_kernel, per_step, n_earlier), grid_...  49.3 us
    ppermute x8, waiting for transfers between devices, halving_scatter(): got = lax.ppermute(sent, 'col', [(i, i ^ stage) for i in range(n_dev)])  34.3 us
    pallas_call x6, Pallas kernels, couple(): pl.pallas_call(functools.partial(couple_kernel, n_columns), grid_spec=plt...  29.4 us
    ppermute x8, starting transfers between devices, halving_scatter(): got = lax.ppermute(sent, 'col', [(i, i ^ stage) for i in range(n_dev)])  22.1 us
    dot_general x17, matrix products, dot_split(): lax.dot_general(high, right, dims, preferred_element_type=F32)  17 us
    dot_general x17, matrix products, dot_split(): lax.dot_general(low, right, dims, preferred_element_type=F32)  14.8 us
    unnamed x74, local copies, waits for them, and re-layouts  12.6 us
  transfers between devices with their start and end apart: 10, of which 5 were waited for; matrix products, arithmetic and copies ran while one was open for 15% of the time, Pallas kernels for 4%

profile of v2, /device:TPU:0, one launch (start us, length us, event | category | flops | bytes accessed | tf_op | source)
XLA Modules:
  0.0 326.1 jit_solution(9465259383419234378)
XLA Ops:
  8.9 2.9 slice_convert_fusion
  22.1 91.3 %all-gather.2.cloned.1.call-done.refs_4_.factor_ref = bf16[3,4096,512]{2,1,0:T(8,128)(2,1)} async-done(((bf16[3,256,512]{2,1,0:T(8,128)(2,1)}), bf16[3,4096,512]{2,1,0:T(8,128)(2,1)}) %all-gather.2.cloned.1.call-update) | async-done | bytes 12582928 | tf_op jit(solution)/shard_map/all_gather | solution.py:150
  113.4 15.1 %fold.3.refs_5_.refs_0_ = f32[1024,512]{1,0:T(8,128)S(1)} custom-call(s32[32]{0:T(128)S(1)} %get-tuple-element.24.list_ref, f32[1024,16384]{1,0:T(8,128)} %refs_3_.5, f32[1024,16384]{1,0:T(8,128)} %refs_3_.5, f32[1024,16384]{1,0:T(8,128)} %refs_3_.5, f32[1024,16384]{1,0:T(8,128)} %refs_3_.5, bf16[3,4096,512]{2,1,0:T(8,128)(2,1)} %all-gather.2.cloned.1.call-done.refs_4_.factor_ref), custom_call_target="tpu_custom_call" | custom-call | tf_op jit(solution)/shard_map/fold/pallas_call | solution.py:65
  128.5 3.5 %couple.6 = f32[1,512,512]{2,1,0:T(8,128)S(1)} custom-call(s32[8]{0:T(128)S(1)} %get-tuple-element.26.place_ref, s32[8]{0:T(128)S(1)} %get-tuple-element.19.present_ref, bf16[3,4096,512]{2,1,0:T(8,128)(2,1)} %all-gather.2.cloned.1.call-done.refs_4_.factor_ref, f32[1024,512]{1,0:T(8,128)S(1)} %fold.3.refs_5_.refs_0_), custom_call_target="tpu_custom_call" | custom-call | tf_op jit(solution)/shard_map/couple/pallas_call | solution.py:101
  134.9 16.0 %fold.4.refs_6_.refs_1_.refs_0_ = f32[1024,512]{1,0:T(8,128)S(1)} custom-call(s32[32]{0:T(128)S(1)} %get-tuple-element.23.list_ref, f32[1024,16384]{1,0:T(8,128)} %refs_3_.5, f32[1024,16384]{1,0:T(8,128)} %refs_3_.5, f32[1024,16384]{1,0:T(8,128)} %refs_3_.5, f32[1024,16384]{1,0:T(8,128)} %refs_3_.5, ...), custom_call_target="tpu_custom_call" | custom-call | tf_op jit(solution)/shard_map/fold/pallas_call | solution.py:65
  150.9 3.7 %couple.8 = f32[1,512,512]{2,1,0:T(8,128)S(1)} custom-call(s32[8]{0:T(128)S(1)} %get-tuple-element.26.place_ref, s32[8]{0:T(128)S(1)} %get-tuple-element.19.present_ref, bf16[3,4096,512]{2,1,0:T(8,128)(2,1)} %all-gather.2.cloned.1.call-done.refs_4_.factor_ref, f32[1024,512]{1,0:T(8,128)S(1)} %fold.4.refs_6_.refs_1_.refs_0_), custom_call_target="tpu_custom_call" | custom-call | tf_op jit(solution)/shard_map/couple/pallas_call | solution.py:101
  156.5 18.2 %fold.5.refs_2_.refs_0_ = f32[1024,512]{1,0:T(8,128)S(1)} custom-call(s32[32]{0:T(128)S(1)} %get-tuple-element.25.list_ref, f32[1024,16384]{1,0:T(8,128)} %refs_3_.5, f32[1024,16384]{1,0:T(8,128)} %refs_3_.5, f32[1024,16384]{1,0:T(8,128)} %refs_3_.5, f32[1024,16384]{1,0:T(8,128)} %refs_3_.5, ...), custom_call_target="tpu_custom_call" | custom-call | tf_op jit(solution)/shard_map/fold/pallas_call | solution.py:65
  174.8 3.7 %couple.10 = f32[1,512,512]{2,1,0:T(8,128)S(1)} custom-call(s32[8]{0:T(128)S(1)} %get-tuple-element.26.place_ref, s32[8]{0:T(128)S(1)} %get-tuple-element.19.present_ref, bf16[3,4096,512]{2,1,0:T(8,128)(2,1)} %all-gather.2.cloned.1.call-done.refs_4_.factor_ref, f32[1024,512]{1,0:T(8,128)S(1)} %fold.5.refs_2_.refs_0_), custom_call_target="tpu_custom_call" | custom-call | tf_op jit(solution)/shard_map/couple/pallas_call | solution.py:101
  180.3 6.3 %couple.7 = f32[2,512,512]{2,1,0:T(8,128)S(1)} custom-call(s32[8]{0:T(128)S(1)} %get-tuple-element.28.place_ref, s32[8]{0:T(128)S(1)} %get-tuple-element.17.present_ref, bf16[3,4096,512]{2,1,0:T(8,128)(2,1)} %all-gather.2.cloned.1.call-done.refs_4_.factor_ref, f32[1024,512]{1,0:T(8,128)S(1)} %fold.3.refs_5_.refs_0_, f32[1024,512]{1,0:T(8,128)} %copy-done), custom_call_target="tpu_custom_call" | custom-call | tf_op jit(solution)/shard_map/couple/pallas_call | solution.py:101
  194.2 8.6 %couple.9 = f32[3,512,512]{2,1,0:T(8,128)} custom-call(s32[8]{0:T(128)S(1)} %get-tuple-element.27.place_ref, s32[8]{0:T(128)S(1)} %get-tuple-element.18.present_ref, bf16[3,4096,512]{2,1,0:T(8,128)(2,1)} %all-gather.2.cloned.1.call-done.refs_4_.factor_ref, f32[1024,512]{1,0:T(8,128)S(1)} %fold.3.refs_5_.refs_0_, f32[1024,512]{1,0:T(8,128)S(1)} %copy-done.1, ...), custom_call_target="tpu_custom_call" | custom-call | tf_op jit(solution)/shard_map/couple/pallas_call | solution.py:101
  202.8 2.7 fusion.9
  207.4 3.5 %couple.11 = f32[1,512,512]{2,1,0:T(8,128)S(1)} custom-call(s32[8]{0:T(128)S(1)} %get-tuple-element.28.place_ref, s32[8]{0:T(128)S(1)} %get-tuple-element.17.present_ref, bf16[3,4096,512]{2,1,0:T(8,128)(2,1)} %all-gather.2.cloned.1.call-done.refs_4_.factor_ref, f32[1024,512]{1,0:T(8,128)S(1)} %copy-done.3), custom_call_target="tpu_custom_call" | custom-call | tf_op jit(solution)/shard_map/couple/pallas_call | solution.py:101
  219.6 2.2 bitcast_add_fusion.1
  222.9 5.0 %collective-permute-start.1 = (f32[3,4,32,512]{3,2,1,0:T(8,128)}, f32[3,4,32,512]{3,2,1,0:T(8,128)}, u32[]{:S(2)}, u32[]{:S(2)}) collective-permute-start(f32[3,4,32,512]{3,2,1,0:T(8,128)} %dynamic-slice_bitcast_fusion.3), channel_id=1, source_target_pairs={{0,2},{1,3},{2,0},{3,1},{4,6},{5,7},{6,4},{7,5},{8,10},{9,11},{10,... | collective-permute-start | bytes 2359304 | tf_op jit(solution)/shard_map/ppermute | solution.py:130
  231.8 2.9 fusion.47
  234.8 11.8 %collective-permute-done.1 = f32[3,4,32,512]{3,2,1,0:T(8,128)} collective-permute-done((f32[3,4,32,512]{3,2,1,0:T(8,128)}, f32[3,4,32,512]{3,2,1,0:T(8,128)}, u32[]{:S(2)}, u32[]{:S(2)}) %collective-permute-start.1) | collective-permute-done | bytes 786464 | tf_op jit(solution)/shard_map/ppermute | solution.py:130
  248.7 14.1 %collective-permute-done.5 = f32[3,4,32,512]{3,2,1,0:T(8,128)} collective-permute-done((f32[3,4,32,512]{3,2,1,0:T(8,128)}, f32[3,4,32,512]{3,2,1,0:T(8,128)}, u32[]{:S(2)}, u32[]{:S(2)}) %collective-permute-start.5) | collective-permute-done | bytes 786464 | tf_op jit(solution)/shard_map/ppermute | solution.py:130
  267.0 2.1 copy.36
  270.3 9.3 %collective-permute-start.3 = (f32[3,1,32,512]{3,2,1,0:T(8,128)S(1)}, f32[3,1,32,512]{3,2,1,0:T(8,128)S(1)}, u32[]{:S(2)}, u32[]{:S(2)}) collective-permute-start(f32[3,1,32,512]{3,2,1,0:T(8,128)S(1)} %constant_dynamic-slice_fusion.1), channel_id=1, source_target_pairs={{0,8},{1,9},{2,10},{3,11},{4,12},{5,13},{6,14},{7,15},{8,0},{9,1},... | collective-permute-start | bytes 589832 | tf_op jit(solution)/shard_map/ppermute | solution.py:130
  280.7 7.7 %collective-permute-start.7 = (f32[3,1,32,512]{3,2,1,0:T(8,128)S(1)}, f32[3,1,32,512]{3,2,1,0:T(8,128)S(1)}, u32[]{:S(2)}, u32[]{:S(2)}) collective-permute-start(f32[3,1,32,512]{3,2,1,0:T(8,128)S(1)} %constant_dynamic-slice_fusion), channel_id=1, source_target_pairs={{0,8},{1,9},{2,10},{3,11},{4,12},{5,13},{6,14},{7,15},{8,0},{9,1},... | collective-permute-start | bytes 589832 | tf_op jit(solution)/shard_map/ppermute | solution.py:130
  290.0 8.4 %collective-permute-done.7 = f32[3,1,32,512]{3,2,1,0:T(8,128)S(1)} collective-permute-done((f32[3,1,32,512]{3,2,1,0:T(8,128)S(1)}, f32[3,1,32,512]{3,2,1,0:T(8,128)S(1)}, u32[]{:S(2)}, u32[]{:S(2)}) %collective-permute-start.7) | collective-permute-done | bytes 196640 | tf_op jit(solution)/shard_map/ppermute | solution.py:130
  301.9 4.0 %all-to-all-start = ((f32[16,1,3072]{2,1,0:T(1,128)}), f32[16,1,3072]{2,1,0:T(1,128)S(1)}, u32[]{:S(2)}, u32[]{:S(2)}) async-start(f32[16,1,3072]{2,1,0:T(1,128)} %reshape.91), calls=%async_computation | async-start | bytes 393216 | tf_op jit(solution)/shard_map/all_to_all | solution.py:199
  305.8 5.7 %pad_maximum_fusion = f32[3,1024,512]{2,1,0:T(8,128)} fusion(f32[1,1024,512]{2,1,0:T(8,128)} %bitcast.243, f32[1,1024,512]{2,1,0:T(8,128)} %bitcast.242, f32[1,1024,512]{2,1,0:T(8,128)S(1)} %bitcast.241), kind=kLoop, calls=%fused_computation | loop fusion | flops 3145728 | bytes 12582912 | tf_op jit(solution)/shard_map/stack | solution.py:205
  311.5 3.3 all-to-all-done
  (158 shorter events, 59.3 us)
Async XLA Ops:
  7.2 106.2 %all-gather.2.cloned.1.call-start = ((), (), s32[]{:S(2)}) async-start(), calls=%async_computation.1 | async-start | bytes 13369344 | tf_op jit(solution)/shard_map/all_gather | solution.py:150
  8.9 4.0 %copy-start.34 = (s32[3,32]{1,0:T(4,128)S(1)}, s32[3,32]{1,0:T(4,128)}, u32[]{:S(2)}) copy-start(s32[3,32]{1,0:T(4,128)} %param.9) | copy-start | bytes 1156
  8.9 4.2 %copy-start.7 = (bf16[3,512,512]{2,1,0:T(8,128)(2,1)S(1)}, bf16[3,512,512]{2,1,0:T(8,128)(2,1)}, u32[]{:S(2)}) copy-start(bf16[3,512,512]{2,1,0:T(8,128)(2,1)} %param.8) | copy-start | bytes 4718596
  128.4 3.6 %copy-start.8 = (bf16[3,512,512]{2,1,0:T(8,128)(2,1)S(1)}, bf16[3,512,512]{2,1,0:T(8,128)(2,1)}, u32[]{:S(2)}) copy-start(bf16[3,512,512]{2,1,0:T(8,128)(2,1)} %param.8) | copy-start | bytes 4718596
  150.9 3.7 %copy-start = (f32[1024,512]{1,0:T(8,128)}, f32[1024,512]{1,0:T(8,128)S(1)}, u32[]{:S(2)}) copy-start(f32[1024,512]{1,0:T(8,128)S(1)} %fold.4.refs_6_.refs_1_.refs_0_) | copy-start | bytes 6291460
  174.8 3.7 %copy-start.2 = (f32[1024,512]{1,0:T(8,128)}, f32[1024,512]{1,0:T(8,128)S(1)}, u32[]{:S(2)}) copy-start(f32[1024,512]{1,0:T(8,128)S(1)} %fold.5.refs_2_.refs_0_) | copy-start | bytes 6291460
  193.4 26.2 %collective-permute-start = (f32[3,8,32,512]{3,2,1,0:T(8,128)}, f32[3,8,32,512]{3,2,1,0:T(8,128)}, u32[]{:S(2)}, u32[]{:S(2)}) collective-permute-start(f32[3,8,32,512]{3,2,1,0:T(8,128)} %dynamic-slice_bitcast_fusion.1), channel_id=1, source_target_pairs={{0,1},{1,0},{2,3},{3,2},{4,5},{5,4},{6,7},{7,6},{8,9},{9,8},{10,11... | collective-permute-start | bytes 4718600 | tf_op jit(solution)/shard_map/ppermute | solution.py:130
  194.2 8.6 %copy-start.20 = (f32[512,512]{1,0:T(8,128)S(1)}, f32[512,512]{1,0:T(8,128)}, u32[]{:S(2)}) copy-start(f32[512,512]{1,0:T(8,128)} %fusion.65) | copy-start | bytes 3145732
  207.4 3.6 %copy-start.24 = (f32[512,512]{1,0:T(8,128)S(1)}, f32[512,512]{1,0:T(8,128)}, u32[]{:S(2)}) copy-start(f32[512,512]{1,0:T(8,128)} %fusion.57) | copy-start | bytes 3145732
  216.5 11.3 %collective-permute-start.4 = (f32[3,8,32,512]{3,2,1,0:T(8,128)S(1)}, f32[3,8,32,512]{3,2,1,0:T(8,128)S(1)}, u32[]{:S(2)}, u32[]{:S(2)}) collective-permute-start(f32[3,8,32,512]{3,2,1,0:T(8,128)S(1)} %dynamic-slice_bitcast_fusion), channel_id=1, source_target_pairs={{0,1},{1,0},{2,3},{3,2},{4,5},{5,4},{6,7},{7,6},{8,9},{9,8},{10,11... | collective-permute-start | bytes 4718600 | tf_op jit(solution)/shard_map/ppermute | solution.py:130
  219.6 10.7 %copy-start.12 = (f32[512,512]{1,0:T(8,128)}, f32[512,512]{1,0:T(8,128)S(1)}, u32[]{:S(2)}) copy-start(f32[512,512]{1,0:T(8,128)S(1)} %fusion.10) | copy-start | bytes 3145732
  221.9 6.4 %copy-start.14 = (f32[3,8,32,512]{3,2,1,0:T(8,128)}, f32[3,8,32,512]{3,2,1,0:T(8,128)S(1)}, u32[]{:S(2)}) copy-start(f32[3,8,32,512]{3,2,1,0:T(8,128)S(1)} %bitcast_add_fusion.1) | copy-start | bytes 4718596
  222.9 23.7 %collective-permute-start.1 = (f32[3,4,32,512]{3,2,1,0:T(8,128)}, f32[3,4,32,512]{3,2,1,0:T(8,128)}, u32[]{:S(2)}, u32[]{:S(2)}) collective-permute-start(f32[3,4,32,512]{3,2,1,0:T(8,128)} %dynamic-slice_bitcast_fusion.3), channel_id=1, source_target_pairs={{0,2},{1,3},{2,0},{3,1},{4,6},{5,7},{6,4},{7,5},{8,10},{9,11},{10,... | collective-permute-start | bytes 2359304 | tf_op jit(solution)/shard_map/ppermute | solution.py:130
  230.3 32.5 %collective-permute-start.5 = (f32[3,4,32,512]{3,2,1,0:T(8,128)}, f32[3,4,32,512]{3,2,1,0:T(8,128)}, u32[]{:S(2)}, u32[]{:S(2)}) collective-permute-start(f32[3,4,32,512]{3,2,1,0:T(8,128)} %dynamic-slice_bitcast_fusion.2), channel_id=1, source_target_pairs={{0,2},{1,3},{2,0},{3,1},{4,6},{5,7},{6,4},{7,5},{8,10},{9,11},{10,... | collective-permute-start | bytes 2359304 | tf_op jit(solution)/shard_map/ppermute | solution.py:130
  231.8 14.7 %copy-start.15 = (f32[3,8,32,512]{3,2,1,0:T(8,128)S(1)}, f32[3,8,32,512]{3,2,1,0:T(8,128)}, u32[]{:S(2)}) copy-start(f32[3,8,32,512]{3,2,1,0:T(8,128)} %copy-done.14) | copy-start | bytes 4718596
  234.8 28.0 %copy-start.17 = (f32[3,8,32,512]{3,2,1,0:T(8,128)S(1)}, f32[3,8,32,512]{3,2,1,0:T(8,128)}, u32[]{:S(2)}) copy-start(f32[3,8,32,512]{3,2,1,0:T(8,128)} %copy-done.16) | copy-start | bytes 4718596
  247.9 16.2 %copy-start.27 = (f32[3,4,32,512]{3,2,1,0:T(8,128)}, f32[3,4,32,512]{3,2,1,0:T(8,128)S(1)}, u32[]{:S(2)}) copy-start(f32[3,4,32,512]{3,2,1,0:T(8,128)S(1)} %bitcast_add_fusion.3) | copy-start | bytes 2359300
  248.7 20.3 %collective-permute-start.2 = (f32[3,2,32,512]{3,2,1,0:T(8,128)}, f32[3,2,32,512]{3,2,1,0:T(8,128)}, u32[]{:S(2)}, u32[]{:S(2)}) collective-permute-start(f32[3,2,32,512]{3,2,1,0:T(8,128)} %dynamic-slice_bitcast_fusion.5), channel_id=1, source_target_pairs={{0,4},{1,5},{2,6},{3,7},{4,0},{5,1},{6,2},{7,3},{8,12},{9,13},{10,... | collective-permute-start | bytes 1179656 | tf_op jit(solution)/shard_map/ppermute | solution.py:130
  265.8 13.8 %collective-permute-start.6 = (f32[3,2,32,512]{3,2,1,0:T(8,128)}, f32[3,2,32,512]{3,2,1,0:T(8,128)}, u32[]{:S(2)}, u32[]{:S(2)}) collective-permute-start(f32[3,2,32,512]{3,2,1,0:T(8,128)} %dynamic-slice_bitcast_fusion.4), channel_id=1, source_target_pairs={{0,4},{1,5},{2,6},{3,7},{4,0},{5,1},{6,2},{7,3},{8,12},{9,13},{10,... | collective-permute-start | bytes 1179656 | tf_op jit(solution)/shard_map/ppermute | solution.py:130
  269.1 10.5 %copy-start.29 = (f32[3,4,32,512]{3,2,1,0:T(8,128)S(1)}, f32[3,4,32,512]{3,2,1,0:T(8,128)}, u32[]{:S(2)}) copy-start(f32[3,4,32,512]{3,2,1,0:T(8,128)} %copy-done.28) | copy-start | bytes 2359300
  270.3 18.1 %collective-permute-start.3 = (f32[3,1,32,512]{3,2,1,0:T(8,128)S(1)}, f32[3,1,32,512]{3,2,1,0:T(8,128)S(1)}, u32[]{:S(2)}, u32[]{:S(2)}) collective-permute-start(f32[3,1,32,512]{3,2,1,0:T(8,128)S(1)} %constant_dynamic-slice_fusion.1), channel_id=1, source_target_pairs={{0,8},{1,9},{2,10},{3,11},{4,12},{5,13},{6,14},{7,15},{8,0},{9,1},... | collective-permute-start | bytes 589832 | tf_op jit(solution)/shard_map/ppermute | solution.py:130
  280.7 17.7 %collective-permute-start.7 = (f32[3,1,32,512]{3,2,1,0:T(8,128)S(1)}, f32[3,1,32,512]{3,2,1,0:T(8,128)S(1)}, u32[]{:S(2)}, u32[]{:S(2)}) collective-permute-start(f32[3,1,32,512]{3,2,1,0:T(8,128)S(1)} %constant_dynamic-slice_fusion), channel_id=1, source_target_pairs={{0,8},{1,9},{2,10},{3,11},{4,12},{5,13},{6,14},{7,15},{8,0},{9,1},... | collective-permute-start | bytes 589832 | tf_op jit(solution)/shard_map/ppermute | solution.py:130
  301.9 12.9 %all-to-all-start = ((f32[16,1,3072]{2,1,0:T(1,128)}), f32[16,1,3072]{2,1,0:T(1,128)S(1)}, u32[]{:S(2)}, u32[]{:S(2)}) async-start(f32[16,1,3072]{2,1,0:T(1,128)} %reshape.91), calls=%async_computation | async-start | bytes 393216 | tf_op jit(solution)/shard_map/all_to_all | solution.py:199
  305.8 5.7 %copy-start.33 = (f32[32,512]{1,0:T(8,128)S(1)}, f32[32,512]{1,0:T(8,128)}, u32[]{:S(2)}) copy-start(f32[32,512]{1,0:T(8,128)} %get-tuple-element.11) | copy-start | bytes 196612
  (21 other events, 33.2 us)
Sparse Core Ops, SparseCore 0:
  10.2 103.1 all-gather.1

commit v3 on v2

--- a/solution.py
+++ b/solution.py
@@ -113,24 +113,15 @@
     )(place, present, factor, *columns)
 
 
-def halving_scatter(value, n_dev):
-    if n_dev & (n_dev - 1):
-        return lax.psum_scatter(value, "col", scatter_dimension=1, tiled=True)
+def halving_stage(value, n_dev, stage):
     count, rows, width = value.shape
-    share = rows // n_dev
-    device = lax.axis_index("col")
-    held = n_dev
-    stage = 1
-    while held > 1:
-        held //= 2
-        parts = value.reshape(count, held, 2, share, width)
-        bit = (device // stage) % 2
-        kept = lax.dynamic_index_in_dim(parts, bit, 2, keepdims=False)
-        sent = lax.dynamic_index_in_dim(parts, 1 - bit, 2, keepdims=False)
-        got = lax.ppermute(sent, "col", [(i, i ^ stage) for i in range(n_dev)])
-        value = kept + got
-        stage *= 2
-    return value.reshape(count, share, width)
+    held = n_dev // (2 * stage)
+    parts = value.reshape(count, held, 2, rows // (2 * held), width)
+    bit = (lax.axis_index("col") // stage) % 2
+    kept = lax.dynamic_index_in_dim(parts, bit, 2, keepdims=False)
+    sent = lax.dynamic_index_in_dim(parts, 1 - bit, 2, keepdims=False)
+    got = lax.ppermute(sent, "col", [(i, i ^ stage) for i in range(n_dev)])
+    return (kept + got).reshape(count, rows // 2, width)
 
 
 def local(separator, pivots, factor_sep, factor_window, block_list):
@@ -171,6 +162,14 @@
         columns.append(
             fold(separator, block_list[k], factors, k, columns[:], [between(k, j) for j in range(k)], block)
         )
+        if k == n_sup - 1:
+            early, columns[k] = lax.optimization_barrier((early, columns[k]))
+            stage = 4
+            while stage < n_dev:
+                early = halving_stage(early, n_dev, stage)
+                stage *= 2
+            for at, pair in enumerate(early_pairs):
+                scattered[pair] = early[at]
         raw = couple(place[k], present[k], factors, k, columns, block)
         for j in range(k):
             sums[k][j] = couple(place[j], present[j], factors, j, [columns[k]], block)[0]
@@ -184,7 +183,17 @@
             sums[j][k] = total
             pending.append((j, k))
         if k >= n_sup - 2:
-            mine = halving_scatter(jnp.stack([sums[j][i] for j, i in pending]), n_dev)
+            mine = jnp.stack([sums[j][i] for j, i in pending])
+            stage = 1
+            if k < n_sup - 1:
+                mine = halving_stage(mine, n_dev, stage)
+                mine, block_list = lax.optimization_barrier((mine, block_list))
+                early, early_pairs = halving_stage(mine, n_dev, 2), pending
+                pending = []
+                continue
+            while stage < n_dev:
+                mine = halving_stage(mine, n_dev, stage)
+                stage *= 2
             for at, pair in enumerate(pending):
                 scattered[pair] = mine[at]
             pending = []

time: 325 us -> 330 us (1.015); the launches traced: 326 us -> 325 us
  matrix products: 31.9 us -> 38.8 us
  starting transfers between devices: 26.1 us -> 19.8 us
  local copies, waits for them, and re-layouts: 21.7 us -> 25.7 us
  waiting for transfers between devices: 129 us -> 125 us
    ppermute x8, waiting for transfers between devices: 34.3 us -> 25.1 us  [halving_stage(): got = lax.ppermute(sent, 'col', [(i, i ^ stage) for i in range(n_dev)])]
    ppermute x8, starting transfers between devices: 22.1 us -> 16.2 us  [halving_stage(): got = lax.ppermute(sent, 'col', [(i, i ^ stage) for i in range(n_dev)])]
    dot_general x17, matrix products: 14.8 us -> 20.6 us  [dot_split(): lax.dot_general(low, right, dims, preferred_element_type=F32)]
    all_gather x1, waiting for transfers between devices: 91.3 us -> 96 us  [local(): factors = lax.all_gather(factor_sep, 'col', axis=1, tiled=True)]
    unnamed x74 -> x92, local copies, waits for them, and re-layouts: 12.6 us -> 15.3 us
  transfers between devices with their start and end apart: 10 -> 10, of which waited for: 5 -> 7; matrix products, arithmetic and copies ran while one was open for 15% -> 14% of each run, Pallas kernels for 4% -> 6%
where the time goes in v3:
time: 330 us; the launch traced here: 325 us
  waiting for transfers between devices  125 us (38%)
  Pallas kernels  78.2 us (24%)
  matrix products  38.8 us (12%)
  local copies, waits for them, and re-layouts  25.7 us (8%)
  other arithmetic  22.9 us (7%)
  starting transfers between devices  19.8 us (6%)
  between operations  14.7 us (4%)
    all_gather x1, waiting for transfers between devices, local(): factors = lax.all_gather(factor_sep, 'col', axis=1, tiled=True)  96 us
    pallas_call x3, Pallas kernels, fold(): pl.pallas_call(functools.partial(fold_kernel, per_step, n_earlier), grid_...  49.6 us
    pallas_call x6, Pallas kernels, couple(): pl.pallas_call(functools.partial(couple_kernel, n_columns), grid_spec=plt...  28.7 us
    ppermute x8, waiting for transfers between devices, halving_stage(): got = lax.ppermute(sent, 'col', [(i, i ^ stage) for i in range(n_dev)])  25.1 us
    dot_general x17, matrix products, dot_split(): lax.dot_general(low, right, dims, preferred_element_type=F32)  20.6 us
    dot_general x17, matrix products, dot_split(): lax.dot_general(high, right, dims, preferred_element_type=F32)  18.2 us
    ppermute x8, starting transfers between devices, halving_stage(): got = lax.ppermute(sent, 'col', [(i, i ^ stage) for i in range(n_dev)])  16.2 us
    unnamed x92, local copies, waits for them, and re-layouts  15.3 us
  transfers between devices with their start and end apart: 10, of which 7 were waited for; matrix products, arithmetic and copies ran while one was open for 14% of the time, Pallas kernels for 6%

profile of v3, /device:TPU:0, one launch (start us, length us, event | category | flops | bytes accessed | tf_op | source)
XLA Modules:
  0.0 325.2 jit_solution(17476447139480156651)
XLA Ops:
  8.9 2.9 slice_convert_fusion
  17.4 96.0 %all-gather.2.cloned.1.call-done.refs_4_.factor_ref = bf16[3,4096,512]{2,1,0:T(8,128)(2,1)} async-done(((bf16[3,256,512]{2,1,0:T(8,128)(2,1)}), bf16[3,4096,512]{2,1,0:T(8,128)(2,1)}) %all-gather.2.cloned.1.call-update) | async-done | bytes 12582928 | tf_op jit(solution)/shard_map/all_gather | solution.py:141
  113.4 15.1 %fold.3.refs_5_.refs_0_ = f32[1024,512]{1,0:T(8,128)S(1)} custom-call(s32[32]{0:T(128)S(1)} %get-tuple-element.31.list_ref, f32[1024,16384]{1,0:T(8,128)} %refs_3_.5, f32[1024,16384]{1,0:T(8,128)} %refs_3_.5, f32[1024,16384]{1,0:T(8,128)} %refs_3_.5, f32[1024,16384]{1,0:T(8,128)} %refs_3_.5, bf16[3,4096,512]{2,1,0:T(8,128)(2,1)} %all-gather.2.cloned.1.call-done.refs_4_.factor_ref), custom_call_target="tpu_custom_call" | custom-call | tf_op jit(solution)/shard_map/fold/pallas_call | solution.py:65
  128.5 16.1 %fold.4.refs_1_.refs_0_.refs_6_ = f32[1024,512]{1,0:T(8,128)S(1)} custom-call(s32[32]{0:T(128)S(1)} %get-tuple-element.32.list_ref, f32[1024,16384]{1,0:T(8,128)} %refs_3_.5, f32[1024,16384]{1,0:T(8,128)} %refs_3_.5, f32[1024,16384]{1,0:T(8,128)} %refs_3_.5, f32[1024,16384]{1,0:T(8,128)} %refs_3_.5, ...), custom_call_target="tpu_custom_call" | custom-call | tf_op jit(solution)/shard_map/fold/pallas_call | solution.py:65
  144.6 4.2 %couple.8 = f32[1,512,512]{2,1,0:T(8,128)S(1)} custom-call(s32[8]{0:T(128)S(1)} %get-tuple-element.33.place_ref, s32[8]{0:T(128)S(1)} %get-tuple-element.27.present_ref, bf16[3,4096,512]{2,1,0:T(8,128)(2,1)} %all-gather.2.cloned.1.call-done.refs_4_.factor_ref, f32[1024,512]{1,0:T(8,128)S(1)} %fold.4.refs_1_.refs_0_.refs_6_), custom_call_target="tpu_custom_call" | custom-call | tf_op jit(solution)/shard_map/couple/pallas_call | solution.py:101
  149.2 3.5 %couple.6 = f32[1,512,512]{2,1,0:T(8,128)S(1)} custom-call(s32[8]{0:T(128)S(1)} %get-tuple-element.33.place_ref, s32[8]{0:T(128)S(1)} %get-tuple-element.27.present_ref, bf16[3,4096,512]{2,1,0:T(8,128)(2,1)} %all-gather.2.cloned.1.call-done.refs_4_.factor_ref, f32[1024,512]{1,0:T(8,128)S(1)} %fold.3.refs_5_.refs_0_), custom_call_target="tpu_custom_call" | custom-call | tf_op jit(solution)/shard_map/couple/pallas_call | solution.py:101
  153.2 5.4 %couple.7 = f32[2,512,512]{2,1,0:T(8,128)S(1)} custom-call(s32[8]{0:T(128)S(1)} %get-tuple-element.34.place_ref, s32[8]{0:T(128)S(1)} %get-tuple-element.26.present_ref, bf16[3,4096,512]{2,1,0:T(8,128)(2,1)} %all-gather.2.cloned.1.call-done.refs_4_.factor_ref, f32[1024,512]{1,0:T(8,128)S(1)} %fold.3.refs_5_.refs_0_, f32[1024,512]{1,0:T(8,128)} %copy-done), custom_call_target="tpu_custom_call" | custom-call | tf_op jit(solution)/shard_map/couple/pallas_call | solution.py:101
  162.7 2.1 collective-permute-start
  180.2 18.4 %fold.5.refs_2_.refs_0_ = f32[1024,512]{1,0:T(8,128)S(1)} custom-call(s32[32]{0:T(128)S(1)} %slice_bitcast_fusion.16.list_ref, f32[1024,16384]{1,0:T(8,128)} %refs_3_.5, f32[1024,16384]{1,0:T(8,128)} %refs_3_.5, f32[1024,16384]{1,0:T(8,128)} %refs_3_.5, f32[1024,16384]{1,0:T(8,128)} %refs_3_.5, ...), custom_call_target="tpu_custom_call" | custom-call | tf_op jit(solution)/shard_map/fold/pallas_call | solution.py:65
  199.8 3.5 %couple.10 = f32[1,512,512]{2,1,0:T(8,128)S(1)} custom-call(s32[8]{0:T(128)S(1)} %get-tuple-element.33.place_ref, s32[8]{0:T(128)S(1)} %get-tuple-element.27.present_ref, bf16[3,4096,512]{2,1,0:T(8,128)(2,1)} %all-gather.2.cloned.1.call-done.refs_4_.factor_ref, f32[1024,512]{1,0:T(8,128)S(1)} %fold.5.refs_2_.refs_0_), custom_call_target="tpu_custom_call" | custom-call | tf_op jit(solution)/shard_map/couple/pallas_call | solution.py:101
  206.8 9.5 %couple.9 = f32[3,512,512]{2,1,0:T(8,128)} custom-call(s32[8]{0:T(128)S(1)} %get-tuple-element.35.place_ref, s32[8]{0:T(128)S(1)} %get-tuple-element.25.present_ref, bf16[3,4096,512]{2,1,0:T(8,128)(2,1)} %all-gather.2.cloned.1.call-done.refs_4_.factor_ref, f32[1024,512]{1,0:T(8,128)S(1)} %fold.3.refs_5_.refs_0_, f32[1024,512]{1,0:T(8,128)S(1)} %copy-done.1, ...), custom_call_target="tpu_custom_call" | custom-call | tf_op jit(solution)/shard_map/couple/pallas_call | solution.py:101
  216.2 3.2 fusion.9
  221.4 2.5 couple.11
  232.5 2.5 fusion.49
  235.0 2.7 fusion.27
  248.1 2.5 collective-permute-start.5
  251.4 5.4 %collective-permute-start.2 = (f32[3,2,32,512]{3,2,1,0:T(8,128)}, f32[3,2,32,512]{3,2,1,0:T(8,128)}, u32[]{:S(2)}, u32[]{:S(2)}) collective-permute-start(f32[3,2,32,512]{3,2,1,0:T(8,128)} %dynamic-slice_bitcast_fusion.5), channel_id=1, source_target_pairs={{0,4},{1,5},{2,6},{3,7},{4,0},{5,1},{6,2},{7,3},{8,12},{9,13},{10,... | collective-permute-start | bytes 1179656 | tf_op jit(solution)/shard_map/ppermute | solution.py:123
  262.0 4.2 %collective-permute-done.2 = f32[3,2,32,512]{3,2,1,0:T(8,128)} collective-permute-done((f32[3,2,32,512]{3,2,1,0:T(8,128)}, f32[3,2,32,512]{3,2,1,0:T(8,128)}, u32[]{:S(2)}, u32[]{:S(2)}) %collective-permute-start.2) | collective-permute-done | bytes 393248 | tf_op jit(solution)/shard_map/ppermute | solution.py:123
  270.3 5.1 %collective-permute-start.6 = (f32[3,2,32,512]{3,2,1,0:T(8,128)S(1)}, f32[3,2,32,512]{3,2,1,0:T(8,128)S(1)}, u32[]{:S(2)}, u32[]{:S(2)}) collective-permute-start(f32[3,2,32,512]{3,2,1,0:T(8,128)S(1)} %dynamic-slice_bitcast_fusion.4), channel_id=1, source_target_pairs={{0,4},{1,5},{2,6},{3,7},{4,0},{5,1},{6,2},{7,3},{8,12},{9,13},{10,... | collective-permute-start | bytes 1179656 | tf_op jit(solution)/shard_map/ppermute | solution.py:123
  278.6 8.3 %collective-permute-done.6 = f32[3,2,32,512]{3,2,1,0:T(8,128)S(1)} collective-permute-done((f32[3,2,32,512]{3,2,1,0:T(8,128)S(1)}, f32[3,2,32,512]{3,2,1,0:T(8,128)S(1)}, u32[]{:S(2)}, u32[]{:S(2)}) %collective-permute-start.6) | collective-permute-done | bytes 393248 | tf_op jit(solution)/shard_map/ppermute | solution.py:123
  288.6 9.4 %collective-permute-done.7 = f32[3,1,32,512]{3,2,1,0:T(8,128)S(1)} collective-permute-done((f32[3,1,32,512]{3,2,1,0:T(8,128)S(1)}, f32[3,1,32,512]{3,2,1,0:T(8,128)S(1)}, u32[]{:S(2)}, u32[]{:S(2)}) %collective-permute-start.7) | collective-permute-done | bytes 196640 | tf_op jit(solution)/shard_map/ppermute | solution.py:123
  301.3 3.6 %all-to-all-start = ((f32[16,1,3072]{2,1,0:T(1,128)}), f32[16,1,3072]{2,1,0:T(1,128)S(1)}, u32[]{:S(2)}, u32[]{:S(2)}) async-start(f32[16,1,3072]{2,1,0:T(1,128)} %reshape.89), calls=%async_computation | async-start | bytes 393216 | tf_op jit(solution)/shard_map/all_to_all | solution.py:208
  304.9 5.7 %pad_maximum_fusion = f32[3,1024,512]{2,1,0:T(8,128)} fusion(f32[1,1024,512]{2,1,0:T(8,128)} %bitcast.245, f32[1,1024,512]{2,1,0:T(8,128)} %bitcast.244, f32[1,1024,512]{2,1,0:T(8,128)S(1)} %bitcast.243), kind=kLoop, calls=%fused_computation | loop fusion | flops 3145728 | bytes 12582912 | tf_op jit(solution)/shard_map/stack | solution.py:214
  310.6 3.3 %all-to-all-done = f32[16,1,3072]{2,1,0:T(1,128)S(1)} async-done(((f32[16,1,3072]{2,1,0:T(1,128)}), f32[16,1,3072]{2,1,0:T(1,128)S(1)}, u32[]{:S(2)}, u32[]{:S(2)}) %all-to-all-start) | async-done | bytes 196640 | tf_op jit(solution)/shard_map/all_to_all | solution.py:208
  (177 shorter events, 75.7 us)
Async XLA Ops:
  7.2 106.2 %all-gather.2.cloned.1.call-start = ((), (), s32[]{:S(2)}) async-start(), calls=%async_computation.1 | async-start | bytes 13369344 | tf_op jit(solution)/shard_map/all_gather | solution.py:141
  8.8 3.3 %copy-start.8 = (bf16[3,512,512]{2,1,0:T(8,128)(2,1)S(1)}, bf16[3,512,512]{2,1,0:T(8,128)(2,1)}, u32[]{:S(2)}) copy-start(bf16[3,512,512]{2,1,0:T(8,128)(2,1)} %param.8) | copy-start | bytes 4718596
  144.5 4.2 %copy-start = (f32[1024,512]{1,0:T(8,128)}, f32[1024,512]{1,0:T(8,128)S(1)}, u32[]{:S(2)}) copy-start(f32[1024,512]{1,0:T(8,128)S(1)} %fold.4.refs_1_.refs_0_.refs_6_) | copy-start | bytes 6291460
  144.5 4.2 %copy-start.9 = (bf16[3,512,512]{2,1,0:T(8,128)(2,1)S(1)}, bf16[3,512,512]{2,1,0:T(8,128)(2,1)}, u32[]{:S(2)}) copy-start(bf16[3,512,512]{2,1,0:T(8,128)(2,1)} %param.8) | copy-start | bytes 4718596
  148.8 9.9 %copy-start.4 = (f32[1,512,512]{2,1,0:T(8,128)}, f32[1,512,512]{2,1,0:T(8,128)S(1)}, u32[]{:S(2)}) copy-start(f32[1,512,512]{2,1,0:T(8,128)S(1)} %couple.8) | copy-start | bytes 3145732
  160.6 4.2 %copy-start.13 = (f32[512,512]{1,0:T(8,128)S(1)}, f32[512,512]{1,0:T(8,128)}, u32[]{:S(2)}) copy-start(f32[512,512]{1,0:T(8,128)} %copy-done.12) | copy-start | bytes 3145732
  162.7 10.9 %collective-permute-start = (f32[3,8,32,512]{3,2,1,0:T(8,128)}, f32[3,8,32,512]{3,2,1,0:T(8,128)}, u32[]{:S(2)}, u32[]{:S(2)}) collective-permute-start(f32[3,8,32,512]{3,2,1,0:T(8,128)} %dynamic-slice_bitcast_fusion.1), channel_id=1, source_target_pairs={{0,1},{1,0},{2,3},{3,2},{4,5},{5,4},{6,7},{7,6},{8,9},{9,8},{10,11... | collective-permute-start | bytes 4718600 | tf_op jit(solution)/shard_map/ppermute | solution.py:123
  177.0 21.6 %collective-permute-start.1 = (f32[3,4,32,512]{3,2,1,0:T(8,128)}, f32[3,4,32,512]{3,2,1,0:T(8,128)S(1)}, u32[]{:S(2)}, u32[]{:S(2)}) collective-permute-start(f32[3,4,32,512]{3,2,1,0:T(8,128)} %dynamic-slice_bitcast_fusion.3), channel_id=1, source_target_pairs={{0,2},{1,3},{2,0},{3,1},{4,6},{5,7},{6,4},{7,5},{8,10},{9,11},{10,... | collective-permute-start | bytes 2359304 | tf_op jit(solution)/shard_map/ppermute | solution.py:123
  198.6 4.8 %copy-start.2 = (f32[1024,512]{1,0:T(8,128)}, f32[1024,512]{1,0:T(8,128)S(1)}, u32[]{:S(2)}) copy-start(f32[1024,512]{1,0:T(8,128)S(1)} %fold.5.refs_2_.refs_0_) | copy-start | bytes 6291460
  216.2 3.2 copy-start.24
  216.2 3.2 copy-start.32
  231.7 3.3 %copy-start.25 = (f32[512,512]{1,0:T(8,128)S(1)}, f32[512,512]{1,0:T(8,128)}, u32[]{:S(2)}) copy-start(f32[512,512]{1,0:T(8,128)} %fusion) | copy-start | bytes 3145732
  231.7 11.7 %collective-permute-start.4 = (f32[3,8,32,512]{3,2,1,0:T(8,128)}, f32[3,8,32,512]{3,2,1,0:T(8,128)}, u32[]{:S(2)}, u32[]{:S(2)}) collective-permute-start(f32[3,8,32,512]{3,2,1,0:T(8,128)} %dynamic-slice_bitcast_fusion), channel_id=1, source_target_pairs={{0,1},{1,0},{2,3},{3,2},{4,5},{5,4},{6,7},{7,6},{8,9},{9,8},{10,11... | collective-permute-start | bytes 4718600 | tf_op jit(solution)/shard_map/ppermute | solution.py:123
  246.0 4.6 %copy-start.37 = (f32[3,4,32,512]{3,2,1,0:T(8,128)S(1)}, f32[3,4,32,512]{3,2,1,0:T(8,128)}, u32[]{:S(2)}) copy-start(f32[3,4,32,512]{3,2,1,0:T(8,128)} %bitcast_add_fusion.3) | copy-start | bytes 2359300
  248.1 20.9 %collective-permute-start.5 = (f32[3,4,32,512]{3,2,1,0:T(8,128)}, f32[3,4,32,512]{3,2,1,0:T(8,128)}, u32[]{:S(2)}, u32[]{:S(2)}) collective-permute-start(f32[3,4,32,512]{3,2,1,0:T(8,128)} %dynamic-slice_bitcast_fusion.2), channel_id=1, source_target_pairs={{0,2},{1,3},{2,0},{3,1},{4,6},{5,7},{6,4},{7,5},{8,10},{9,11},{10,... | collective-permute-start | bytes 2359304 | tf_op jit(solution)/shard_map/ppermute | solution.py:123
  251.4 14.8 %collective-permute-start.2 = (f32[3,2,32,512]{3,2,1,0:T(8,128)}, f32[3,2,32,512]{3,2,1,0:T(8,128)}, u32[]{:S(2)}, u32[]{:S(2)}) collective-permute-start(f32[3,2,32,512]{3,2,1,0:T(8,128)} %dynamic-slice_bitcast_fusion.5), channel_id=1, source_target_pairs={{0,4},{1,5},{2,6},{3,7},{4,0},{5,1},{6,2},{7,3},{8,12},{9,13},{10,... | collective-permute-start | bytes 1179656 | tf_op jit(solution)/shard_map/ppermute | solution.py:123
  260.0 6.2 %copy-start.38 = (f32[3,4,32,512]{3,2,1,0:T(8,128)S(1)}, f32[3,4,32,512]{3,2,1,0:T(8,128)}, u32[]{:S(2)}) copy-start(f32[3,4,32,512]{3,2,1,0:T(8,128)} %bitcast_add_fusion.3) | copy-start | bytes 2359300
  260.0 9.0 %copy-start.30 = (f32[3,8,32,512]{3,2,1,0:T(8,128)S(1)}, f32[3,8,32,512]{3,2,1,0:T(8,128)}, u32[]{:S(2)}) copy-start(f32[3,8,32,512]{3,2,1,0:T(8,128)} %copy-done.29) | copy-start | bytes 4718596
  267.2 8.2 %copy-start.27 = (f32[512,512]{1,0:T(8,128)S(1)}, f32[512,512]{1,0:T(8,128)}, u32[]{:S(2)}) copy-start(f32[512,512]{1,0:T(8,128)} %fusion.10) | copy-start | bytes 3145732
  267.3 11.3 %collective-permute-start.3 = (f32[3,1,32,512]{3,2,1,0:T(8,128)S(1)}, f32[3,1,32,512]{3,2,1,0:T(8,128)S(1)}, u32[]{:S(2)}, u32[]{:S(2)}) collective-permute-start(f32[3,1,32,512]{3,2,1,0:T(8,128)S(1)} %constant_dynamic-slice_fusion.1), channel_id=1, source_target_pairs={{0,8},{1,9},{2,10},{3,11},{4,12},{5,13},{6,14},{7,15},{8,0},{9,1},... | collective-permute-start | bytes 589832 | tf_op jit(solution)/shard_map/ppermute | solution.py:123
  270.3 16.6 %collective-permute-start.6 = (f32[3,2,32,512]{3,2,1,0:T(8,128)S(1)}, f32[3,2,32,512]{3,2,1,0:T(8,128)S(1)}, u32[]{:S(2)}, u32[]{:S(2)}) collective-permute-start(f32[3,2,32,512]{3,2,1,0:T(8,128)S(1)} %dynamic-slice_bitcast_fusion.4), channel_id=1, source_target_pairs={{0,4},{1,5},{2,6},{3,7},{4,0},{5,1},{6,2},{7,3},{8,12},{9,13},{10,... | collective-permute-start | bytes 1179656 | tf_op jit(solution)/shard_map/ppermute | solution.py:123
  287.0 11.0 %collective-permute-start.7 = (f32[3,1,32,512]{3,2,1,0:T(8,128)S(1)}, f32[3,1,32,512]{3,2,1,0:T(8,128)S(1)}, u32[]{:S(2)}, u32[]{:S(2)}) collective-permute-start(f32[3,1,32,512]{3,2,1,0:T(8,128)S(1)} %constant_dynamic-slice_fusion), channel_id=1, source_target_pairs={{0,8},{1,9},{2,10},{3,11},{4,12},{5,13},{6,14},{7,15},{8,0},{9,1},... | collective-permute-start | bytes 589832 | tf_op jit(solution)/shard_map/ppermute | solution.py:123
  301.3 12.6 %all-to-all-start = ((f32[16,1,3072]{2,1,0:T(1,128)}), f32[16,1,3072]{2,1,0:T(1,128)S(1)}, u32[]{:S(2)}, u32[]{:S(2)}) async-start(f32[16,1,3072]{2,1,0:T(1,128)} %reshape.89), calls=%async_computation | async-start | bytes 393216 | tf_op jit(solution)/shard_map/all_to_all | solution.py:208
  304.9 5.7 %copy-start.42 = (f32[32,512]{1,0:T(8,128)S(1)}, f32[32,512]{1,0:T(8,128)}, u32[]{:S(2)}) copy-start(f32[32,512]{1,0:T(8,128)} %get-tuple-element.19) | copy-start | bytes 196612
  (30 other events, 51.4 us)
Sparse Core Ops, SparseCore 0:
  10.2 103.1 all-gather.1
